TPU v7x, 32 devices: a whole 2x2x4 slice. The times are simulated.
32 devices in a mesh: grp: 2 (over y), pos: 16 (over z, x, core).
Axes of the slice: x: 2, y: 2, z: 4, core: 2. Of those that a mesh axis runs over, the one named last changes fastest.
Arguments:
- object_field: float32 [2, 2048, 2048], P(None, 'grp', 'pos'), may hold values from -5 to 5
- probe_field: float32 [2, 256, 256], replicated, may hold values from -5 to 5
- patterns: float32 [96, 256, 256], P(('grp', 'pos')), may hold values from 0.05 to 5
- corners: int32 [2, 96], P(None, ('grp', 'pos')), may hold values from 0 to 1792, as said below
- counts: int32 [32], replicated, may hold values from 1 to 3, as said below
Outputs:
- object_new: float32 [2, 2048, 2048], P(None, 'grp', 'pos')
- probe_new: float32 [2, 256, 256], replicated
Inputs may be any that keep to these rules, and one draw needn't show every extreme that they name: `corners`: each slot's patch of 256 x 256 cells lies inside the object and inside its device's block of 1024 x 128 object cells extended by 128 cells on every side (the device at grp index a and pos index b holds rows a * 1024 to a * 1024 + 1023 and columns b * 128 to b * 128 + 127). The live slots of a device are its first counts[d] slots; some device has all 3 slots live.
All inputs are finite; a program needn't handle non-finite values.
Results may differ from a plain program's by a relative error of at most 0.00012.
Values sent between devices are 32-bit elements; how exact they have to be, the bound alone decides.
A program may use at most 64 MiB of HBM per device.

v0:
```python
import math
import jax
import jax.numpy as jnp
from jax import lax
from jax.sharding import PartitionSpec as P

M = 256
HALO = 128
step_object = 0.25
step_probe = 4.0


def padded(x, sides, width):
    for axis, dim in sides:
        peers, length = (lax.axis_size(axis), x.shape[dim])
        up = [(i, (i + 1) % peers) for i in range(peers - 1)]
        down = [(j, i) for i, j in up]
        last = lax.slice_in_dim(x, length - width, length, axis=dim)
        initial = lax.slice_in_dim(x, 0, width, axis=dim)
        before = lax.ppermute(last, axis, up)
        after = lax.ppermute(initial, axis, down)
        x = jnp.concatenate([before, x, after], axis=dim)
    return x


def product(left, right):
    return jnp.dot(left, right, precision=lax.Precision.HIGHEST, preferred_element_type=jnp.float32)


def left_mul(cos_part, sin_part, real_part, imag_part):
    return (
        product(cos_part, real_part) - product(sin_part, imag_part),
        product(cos_part, imag_part) + product(sin_part, real_part),
    )


def right_mul(real_part, imag_part, cos_part, sin_part):
    return (
        product(real_part, cos_part) - product(imag_part, sin_part),
        product(real_part, sin_part) + product(imag_part, cos_part),
    )


def dft_tables(order):
    indices = jnp.arange(order, dtype=jnp.int32)
    phases = indices[:, None] * indices[None, :] % order
    angles = phases.astype(jnp.float32) * (2.0 * math.pi / order)
    factor = 1.0 / math.sqrt(order)
    return (jnp.cos(angles) * factor, -jnp.sin(angles) * factor)


def far_field(wave, measured, cos_table, sin_table):
    front_re, front_im = left_mul(cos_table, sin_table, wave[0], wave[1])
    far_re, far_im = right_mul(front_re, front_im, cos_table, sin_table)
    excess = far_re * far_re + far_im * far_im - measured
    back_re, back_im = left_mul(cos_table, -sin_table, excess * far_re, excess * far_im)
    chi_re, chi_im = right_mul(back_re, back_im, cos_table, -sin_table)
    return jnp.stack((chi_re, chi_im))


def on_device(object_field, probe_field, patterns, corners, counts):
    tile_rows = object_field.shape[1]
    tile_cols = object_field.shape[2]
    slot_count = patterns.shape[0]
    pos_count = lax.axis_size("pos")
    grp_index = lax.axis_index("grp")
    pos_index = lax.axis_index("pos")
    device = grp_index * pos_count + pos_index
    own_count = counts[device]
    cos_table, sin_table = dft_tables(M)
    extended = padded(object_field, (("grp", 1), ("pos", 2)), HALO)
    row_local = corners[0] - grp_index * tile_rows + HALO
    col_local = corners[1] - pos_index * tile_cols + HALO

    def cut_patch(row_at, col_at):
        return lax.dynamic_slice(extended, (jnp.int32(0), row_at, col_at), (2, M, M))

    patches = jax.vmap(cut_patch)(row_local, col_local)
    waves = jnp.stack(
        (
            probe_field[0] * patches[:, 0] - probe_field[1] * patches[:, 1],
            probe_field[0] * patches[:, 1] + probe_field[1] * patches[:, 0],
        ),
        axis=1,
    )
    empty_results = jnp.zeros((slot_count, 2, M, M), jnp.float32)

    def solve_own(step, results):
        result = far_field(waves[step], patterns[step], cos_table, sin_table)
        return lax.dynamic_update_index_in_dim(results, result, step, 0)

    residuals = lax.fori_loop(0, own_count, solve_own, empty_results)

    def accumulate(step, totals):
        grad_ext, grad_probe = totals
        chi_re = residuals[step, 0]
        chi_im = residuals[step, 1]
        patch_re = patches[step, 0]
        patch_im = patches[step, 1]
        obj_part = jnp.stack(
            (
                probe_field[0] * chi_re + probe_field[1] * chi_im,
                probe_field[0] * chi_im - probe_field[1] * chi_re,
            )
        )
        prb_part = jnp.stack(
            (patch_re * chi_re + patch_im * chi_im, patch_re * chi_im - patch_im * chi_re)
        )
        anchor = (jnp.int32(0), row_local[step], col_local[step])
        current = lax.dynamic_slice(grad_ext, anchor, (2, M, M))
        grad_ext = lax.dynamic_update_slice(grad_ext, current + obj_part, anchor)
        return (grad_ext, grad_probe + prb_part)

    start_totals = (
        jnp.zeros(extended.shape, jnp.float32),
        jnp.zeros(probe_field.shape, jnp.float32),
    )
    grad_ext, grad_probe = lax.fori_loop(0, own_count, accumulate, start_totals)
    col_rims = jnp.concatenate((grad_ext[:, :, :HALO], grad_ext[:, :, -HALO:]), axis=2)
    col_arrived = padded(col_rims, (("pos", 2),), HALO)
    middle = grad_ext[:, :, HALO : HALO + tile_cols]
    middle = middle.at[:, :, :HALO].add(col_arrived[:, :, :HALO])
    middle = middle.at[:, :, tile_cols - HALO :].add(col_arrived[:, :, -HALO:])
    row_rims = jnp.concatenate((middle[:, :HALO], middle[:, -HALO:]), axis=1)
    row_arrived = padded(row_rims, (("grp", 1),), HALO)
    core = middle[:, HALO : HALO + tile_rows]
    core = core.at[:, :HALO].add(row_arrived[:, :HALO])
    core = core.at[:, tile_rows - HALO :].add(row_arrived[:, -HALO:])
    object_new = object_field - step_object * core
    live_total = jnp.sum(counts).astype(jnp.float32)
    share = lax.psum_scatter(grad_probe, "pos", scatter_dimension=1, tiled=True)
    share = lax.psum(share, "grp")
    row_share = M // pos_count
    mine = lax.dynamic_slice_in_dim(probe_field, pos_index * row_share, row_share, 1)
    new_rows = mine - step_probe * share / live_total
    probe_new = lax.all_gather(new_rows, "pos", axis=1, tiled=True)
    return (object_new, probe_new)


def solution(mesh):
    return jax.shard_map(
        on_device,
        mesh=mesh,
        in_specs=(
            P(None, "grp", "pos"),
            P(),
            P(("grp", "pos"), None, None),
            P(None, ("grp", "pos")),
            P(),
        ),
        out_specs=(P(None, "grp", "pos"), P()),
        check_vma=False,
    )
```

profile of v0, /device:TPU:0, one launch (start us, length us, event | category | flops | bytes accessed | tf_op | source)
XLA Modules:
  0.0 322.7 jit_solution(2919764576730867751)
XLA Ops:
  8.3 4.9 %collective-permute-start = (f32[2,128,128]{2,1,0:T(8,128)S(1)}, f32[2,128,128]{2,1,0:T(8,128)S(1)}, u32[]{:S(2)}, u32[]{:S(2)}) collective-permute-start(f32[2,128,128]{2,1,0:T(8,128)S(1)} %get-tuple-element.348), channel_id=1, source_target_pairs={{0,16},{1,17},{2,18},{3,19},{4,20},{5,21},{6,22},{7,23},{8,24},{9,... | collective-permute-start | bytes 393224 | tf_op jit(solution)/shard_map/ppermute | solution.py:20
  13.2 1.3 collective-permute-start.1
  14.5 1.4 collective-permute-done
  15.9 1.3 constant_dynamic-update-slice_fusion.1
  17.2 2.8 collective-permute-done.1
  20.1 1.4 collective-permute-start.2
  21.5 1.3 collective-permute-start.3
  24.4 3.7 %collective-permute-done.3 = f32[2,1280,128]{2,1,0:T(8,128)} collective-permute-done((f32[2,1280,128]{2,1,0:T(8,128)S(1)}, f32[2,1280,128]{2,1,0:T(8,128)}, u32[]{:S(2)}, u32[]{:S(2)}) %collective-permute-start.3) | collective-permute-done | bytes 1310752 | tf_op jit(solution)/shard_map/ppermute | solution.py:21
  28.2 3.4 %pad_maximum_fusion = f32[2,1280,384]{2,1,0:T(8,128)} fusion(f32[2,1280,128]{2,1,0:T(8,128)} %collective-permute-done.3, f32[2,1280,128]{2,1,0:T(8,128)S(1)} %constant_dynamic-update-slice_fusion, f32[2,1280,128]{2,1,0:T(8,128)S(1)} %collective-permute-done.2), kind=kLoop, calls=%fused_computation.139 | loop fusion | flops 1966080 | bytes 7864320 | tf_op jit(solution)/shard_map/concatenate | solution.py:22
  31.8 9.6 %while.33 = (s32[]{:T(128)}, f32[2,1280,384]{2,1,0:T(8,128)}, s32[3,3]{1,0:T(4,128)S(1)}, f32[3,2,256,256]{3,2,1,0:T(8,128)S(1)}, s32[]{:T(128)}) while((s32[]{:T(128)}, f32[2,1280,384]{2,1,0:T(8,128)}, s32[3,3]{1,0:T(4,128)S(1)}, f32[3,2,256,256]{3,2,1,0:T(8,128)S(1)}, s32[]{:T(128)}) %tuple.101), condition=%wide.while_cond.4, body=%wide.while_body.4.sunk | while | flops 2 | bytes 1048693 | solution.py:76
  32.4 2.5 bitcast_dynamic-update-slice_fusion.2
  35.7 2.5 bitcast_dynamic-update-slice_fusion.2
  38.9 2.5 bitcast_dynamic-update-slice_fusion.2
  41.6 1.3 pad_maximum_fusion.1
  42.9 1.3 broadcast_in_dim.20
  44.2 30.9 %while.34 = (s32[]{:T(128)}, f32[3,2,256,256]{3,2,1,0:T(8,128)}, s32[]{:T(128)}, f32[3,2,256,256]{3,2,1,0:T(8,128)}, f32[3,256,256]{2,1,0:T(8,128)}, /*index=5*/s32[]{:T(128)}, s32[]{:T(128)}, s32[]{:T(128)}, s32[]{}) while((s32[]{:T(128)}, f32[3,2,256,256]{3,2,1,0:T(8,128)}, s32[]{:T(128)}, ...), condition=%wide.region_1.2_spmd.clone.clone, body=%wide.region_0.1_spmd.clone.clone.sunk | while | flops 3238789120 | bytes 12320939 | solution.py:92
  44.9 2.4 fusion.179
  47.3 2.4 convolution_subtract_fusion.7
  49.8 1.5 fusion.180
  51.2 2.4 fusion.181
  53.7 2.4 convolution_add_fusion.6
  56.1 1.5 convolution_subtract_fusion.8
  57.6 1.5 fusion.182
  59.1 2.4 fusion.183
  61.5 1.5 fusion.186
  63.0 1.5 convolution_add_fusion.7
  64.5 1.5 fusion.184
  66.0 1.5 convolution_subtract_fusion.9
  67.5 1.5 fusion.188
  68.9 1.5 fusion.189
  70.4 1.5 fusion.185
  71.9 1.5 fusion.187
  75.1 2.1 broadcast_in_dim.18
  77.3 14.2 %while.32 = (s32[]{:T(128)}, f32[2,1280,384]{2,1,0:T(8,128)}, f32[2,256,256]{2,1,0:T(8,128)S(1)}, s32[]{:T(128)}, s32[3]{0:T(128)S(1)}, /*index=5*/s32[3]{0:T(12...) while((s32[]{:T(128)}, f32[2,1280,384]{2,1,0:T(8,128)}, ...), condition=%wide.region_3.4_spmd, body=%wide.region_2.3_spmd.sunk | while | flops 1310731 | bytes 6816019 | solution.py:118
  83.1 1.1 fusion.161
  84.2 1.4 maximum_add_fusion.3
  85.6 5.2 %dynamic_update_slice.13 = f32[2,1280,384]{2,1,0:T(8,128)} dynamic-update-slice(f32[2,1280,384]{2,1,0:T(8,128)} %get-tuple-element.545, f32[2,256,256]{2,1,0:T(8,128)S(1)} %get-tuple-element.473, s32[]{:T(128)} %constant.180.clone.1..sunk, s32[]{:T(128)S(6)} %select_n.163, s32[]{:T(128)S(6)} %select_n.164) | dynamic-update-slice | bytes 1048580 | tf_op jit(solution)/shard_map/while/body/dynamic_update_slice | solution.py:111
  91.5 3.2 fusion.116
  94.7 27.6 %collective-permute-start.4 = (f32[2,1280,128]{2,1,0:T(8,128)}, f32[2,1280,128]{2,1,0:T(8,128)S(1)}, u32[]{:S(2)}, u32[]{:S(2)}) collective-permute-start(f32[2,1280,128]{2,1,0:T(8,128)} %get-tuple-element.341), channel_id=1, source_target_pairs={{0,1},{1,2},{2,3},{3,4},{4,5},{5,6},{6,7},{7,8},{8,9},{9,10},{10,1... | collective-permute-start | bytes 3932168 | tf_op jit(solution)/shard_map/ppermute | solution.py:20
  122.3 1.3 collective-permute-start.5
  124.9 147.0 %reduce-scatter.2.cloned.1.call-done = f32[2,16,256]{2,1,0:T(8,128)} async-done(((f32[2,256,256]{2,1,0:T(8,128)}), f32[2,16,256]{2,1,0:T(8,128)}) %reduce-scatter.2.cloned.1.call-update) | async-done | bytes 32784 | tf_op jit(solution)/shard_map/reduce_scatter | solution.py:131
  271.9 9.0 %psum.7 = f32[2,16,256]{2,1,0:T(8,128)S(1)} all-reduce(f32[2,16,256]{2,1,0:T(8,128)} %reduce-scatter.2.cloned.1.call-done), channel_id=1, replica_groups=mesh['grp'=2,'pos'=16] {'grp'}, use_global_device_ids=true, to_apply=%region_5.6 | all-reduce | flops 8192 | bytes 65536 | tf_op jit(solution)/shard_map/psum | solution.py:132
  280.9 1.9 add_add_fusion
  282.8 2.5 collective-permute-start.6
  285.3 20.9 %all_gather.3 = f32[2,256,256]{2,1,0:T(8,128)S(1)} all-gather(f32[2,16,256]{2,1,0:T(8,128)S(1)} %divide_subtract_fusion), channel_id=1, replica_groups=mesh['grp'=2,'pos'=16] {'pos'}, dimensions={1}, use_global_device_ids=true | all-gather | bytes 557056 | tf_op jit(solution)/shard_map/all_gather | solution.py:136
  306.2 1.4 collective-permute-start.7
  307.7 6.3 %collective-permute-done.7 = f32[2,128,128]{2,1,0:T(8,128)S(1)} collective-permute-done((f32[2,128,128]{2,1,0:T(8,128)S(1)}, f32[2,128,128]{2,1,0:T(8,128)S(1)}, u32[]{:S(2)}, u32[]{:S(2)}) %collective-permute-start.7) | collective-permute-done | bytes 131104 | tf_op jit(solution)/shard_map/ppermute | solution.py:21
  314.0 1.1 multiply_subtract_fusion
  (49 shorter events, 8.7 us)
Async XLA Ops:
  7.2 15.6 %copy-start.5 = (s32[2,3]{1,0:T(2,128)S(1)}, s32[2,3]{1,0:T(2,128)}, u32[]{:S(2)}) copy-start(s32[2,3]{1,0:T(2,128)} %param.24) | copy-start | bytes 76
  7.2 15.7 %copy-start.6 = (s32[32]{0:T(128)S(1)}, s32[32]{0:T(128)}, u32[]{:S(2)}) copy-start(s32[32]{0:T(128)} %param.25) | copy-start | bytes 388
  7.2 16.4 %copy-start.1 = (f32[2,256,256]{2,1,0:T(8,128)S(1)}, f32[2,256,256]{2,1,0:T(8,128)}, u32[]{:S(2)}) copy-start(f32[2,256,256]{2,1,0:T(8,128)} %param.22) | copy-start | bytes 1572868
  7.2 264.7 %reduce-scatter.2.cloned.1.call-start = ((), (), s32[]{:S(2)}) async-start(), calls=%async_computation.1 | async-start | bytes 557056 | tf_op jit(solution)/shard_map/reduce_scatter | solution.py:131
  8.3 7.6 %collective-permute-start = (f32[2,128,128]{2,1,0:T(8,128)S(1)}, f32[2,128,128]{2,1,0:T(8,128)S(1)}, u32[]{:S(2)}, u32[]{:S(2)}) collective-permute-start(f32[2,128,128]{2,1,0:T(8,128)S(1)} %get-tuple-element.348), channel_id=1, source_target_pairs={{0,16},{1,17},{2,18},{3,19},{4,20},{5,21},{6,22},{7,23},{8,24},{9,... | collective-permute-start | bytes 393224 | tf_op jit(solution)/shard_map/ppermute | solution.py:20
  13.2 6.9 %collective-permute-start.1 = (f32[2,128,128]{2,1,0:T(8,128)S(1)}, f32[2,128,128]{2,1,0:T(8,128)S(1)}, u32[]{:S(2)}, u32[]{:S(2)}) collective-permute-start(f32[2,128,128]{2,1,0:T(8,128)S(1)} %get-tuple-element.347), channel_id=1, source_target_pairs={{16,0},{17,1},{18,2},{19,3},{20,4},{21,5},{22,6},{23,7},{24,8},{25... | collective-permute-start | bytes 393224 | tf_op jit(solution)/shard_map/ppermute | solution.py:21
  20.1 4.3 %collective-permute-start.2 = (f32[2,1280,128]{2,1,0:T(8,128)S(1)}, f32[2,1280,128]{2,1,0:T(8,128)S(1)}, u32[]{:S(2)}, u32[]{:S(2)}) collective-permute-start(f32[2,1280,128]{2,1,0:T(8,128)S(1)} %constant_dynamic-update-slice_fusion), channel_id=1, source_target_pairs={{0,1},{1,2},{2,3},{3,4},{4,5},{5,6},{6,7},{7,8},{8,9},{9,10},{10,1... | collective-permute-start | bytes 3932168 | tf_op jit(solution)/shard_map/ppermute | solution.py:20
  21.5 6.7 %collective-permute-start.3 = (f32[2,1280,128]{2,1,0:T(8,128)S(1)}, f32[2,1280,128]{2,1,0:T(8,128)}, u32[]{:S(2)}, u32[]{:S(2)}) collective-permute-start(f32[2,1280,128]{2,1,0:T(8,128)S(1)} %constant_dynamic-update-slice_fusion), channel_id=1, source_target_pairs={{1,0},{2,1},{3,2},{4,3},{5,4},{6,5},{7,6},{8,7},{9,8},{10,9},{11,1... | collective-permute-start | bytes 3932168 | tf_op jit(solution)/shard_map/ppermute | solution.py:21
  31.7 9.7 %copy-start.3 = (f32[256,256]{1,0:T(8,128)S(1)}, f32[256,256]{1,0:T(8,128)}, u32[]{:S(2)}) copy-start(f32[256,256]{1,0:T(8,128)} %get-tuple-element.349) | copy-start | bytes 786436
  31.7 9.7 %copy-start.4 = (f32[256,256]{1,0:T(8,128)S(1)}, f32[256,256]{1,0:T(8,128)}, u32[]{:S(2)}) copy-start(f32[256,256]{1,0:T(8,128)} %get-tuple-element.350) | copy-start | bytes 786436
  91.5 3.2 copy-start
  94.7 186.2 %collective-permute-start.4 = (f32[2,1280,128]{2,1,0:T(8,128)}, f32[2,1280,128]{2,1,0:T(8,128)S(1)}, u32[]{:S(2)}, u32[]{:S(2)}) collective-permute-start(f32[2,1280,128]{2,1,0:T(8,128)} %get-tuple-element.341), channel_id=1, source_target_pairs={{0,1},{1,2},{2,3},{3,4},{4,5},{5,6},{6,7},{7,8},{8,9},{9,10},{10,1... | collective-permute-start | bytes 3932168 | tf_op jit(solution)/shard_map/ppermute | solution.py:20
  122.3 158.6 %collective-permute-start.5 = (f32[2,1280,128]{2,1,0:T(8,128)S(1)}, f32[2,1280,128]{2,1,0:T(8,128)}, u32[]{:S(2)}, u32[]{:S(2)}) collective-permute-start(f32[2,1280,128]{2,1,0:T(8,128)S(1)} %get-tuple-element.342), channel_id=1, source_target_pairs={{1,0},{2,1},{3,2},{4,3},{5,4},{6,5},{7,6},{8,7},{9,8},{10,9},{11,1... | collective-permute-start | bytes 3932168 | tf_op jit(solution)/shard_map/ppermute | solution.py:21
  282.8 24.8 %collective-permute-start.6 = (f32[2,128,128]{2,1,0:T(8,128)S(1)}, f32[2,128,128]{2,1,0:T(8,128)S(1)}, u32[]{:S(2)}, u32[]{:S(2)}) collective-permute-start(f32[2,128,128]{2,1,0:T(8,128)S(1)} %get-tuple-element.346), channel_id=1, source_target_pairs={{0,16},{1,17},{2,18},{3,19},{4,20},{5,21},{6,22},{7,23},{8,24},{9,... | collective-permute-start | bytes 393224 | tf_op jit(solution)/shard_map/ppermute | solution.py:20
  306.1 7.9 %copy-start.2 = (f32[2,1024,128]{2,1,0:T(8,128)S(1)}, f32[2,1024,128]{2,1,0:T(8,128)}, u32[]{:S(2)}) copy-start(f32[2,1024,128]{2,1,0:T(8,128)} %param.21) | copy-start | bytes 3145732
  306.2 7.8 %collective-permute-start.7 = (f32[2,128,128]{2,1,0:T(8,128)S(1)}, f32[2,128,128]{2,1,0:T(8,128)S(1)}, u32[]{:S(2)}, u32[]{:S(2)}) collective-permute-start(f32[2,128,128]{2,1,0:T(8,128)S(1)} %get-tuple-element.345), channel_id=1, source_target_pairs={{16,0},{17,1},{18,2},{19,3},{20,4},{21,5},{22,6},{23,7},{24,8},{25... | collective-permute-start | bytes 393224 | tf_op jit(solution)/shard_map/ppermute | solution.py:21
Sparse Core Ops, SparseCore 0:
  123.8 148.0 reduce-scatter.1
where the time goes:
time: 325 us; the launch traced here: 323 us
  waiting for transfers between devices  161 us (50%)
  starting transfers between devices  41.7 us (13%)
  blocking collectives  29.8 us (9%)
  matrix products  28.4 us (9%)
  local copies, waits for them, and re-layouts  27.6 us (8%)
  between operations  15 us (5%)
  other arithmetic  11.9 us (4%)
  loops' own time  7.08 us (2%)
    reduce_scatter x1, waiting for transfers between devices, on_device(): share = lax.psum_scatter(grad_probe, 'pos', scatter_dimension=1, tiled=True)  147 us
    ppermute x4, starting transfers between devices, padded(): before = lax.ppermute(last, axis, up)  36.3 us
    dot_general x16, matrix products, product(): jnp.dot(left, right, precision=lax.Precision.HIGHEST, preferred_element_t...  28.4 us
    all_gather x1, blocking collectives, on_device(): probe_new = lax.all_gather(new_rows, 'pos', axis=1, tiled=True)  20.9 us
    ppermute x4, waiting for transfers between devices, padded(): after = lax.ppermute(initial, axis, down)  12.9 us
    gather x9, local copies, waits for them, and re-layouts  9.58 us
    psum x1, blocking collectives, on_device(): share = lax.psum(share, 'grp')  8.97 us
  transfers between devices with their start and end apart: 9, of which 5 were waited for; matrix products, arithmetic and copies ran while one was open for 1% of the time, Pallas kernels for 0%

commit v1 on v0

--- a/solution.py
+++ b/solution.py
@@ -1,3 +1,4 @@
+import functools
 import math
 import jax
 import jax.numpy as jnp
@@ -8,6 +9,15 @@
 HALO = 128
 step_object = 0.25
 step_probe = 4.0
+
+
+def try_all_wall(inp, mesh_ax):
+    lower = lax.all_gather(inp, mesh_ax)
+    current_block = jnp.concatenate(lower, axis=1)
+    return current_block
+
+
+apply_terms_all = functools.partial(try_all_wall, mesh_ax="pos")
 
 
 def padded(x, sides, width):
@@ -133,7 +143,7 @@
     row_share = M // pos_count
     mine = lax.dynamic_slice_in_dim(probe_field, pos_index * row_share, row_share, 1)
     new_rows = mine - step_probe * share / live_total
-    probe_new = lax.all_gather(new_rows, "pos", axis=1, tiled=True)
+    probe_new = apply_terms_all(new_rows)
     return (object_new, probe_new)
 
 

time: 325 us -> 324 us (level)
  no operation moved by 1% of the time
where the time goes in v1:
time: 324 us; the launch traced here: 322 us
  waiting for transfers between devices  161 us (50%)
  starting transfers between devices  41.7 us (13%)
  blocking collectives  29.8 us (9%)
  matrix products  28.3 us (9%)
  local copies, waits for them, and re-layouts  27.9 us (9%)
  between operations  15 us (5%)
  other arithmetic  11.6 us (4%)
  loops' own time  6.58 us (2%)
    reduce_scatter x1, waiting for transfers between devices, on_device(): share = lax.psum_scatter(grad_probe, 'pos', scatter_dimension=1, tiled=True)  146 us
    ppermute x4, starting transfers between devices, padded(): before = lax.ppermute(last, axis, up)  36.3 us
    dot_general x16, matrix products, product(): jnp.dot(left, right, precision=lax.Precision.HIGHEST, preferred_element_t...  28.3 us
    all_gather x1, blocking collectives, try_all_wall(): lower = lax.all_gather(inp, mesh_ax)  20.9 us
    ppermute x4, waiting for transfers between devices, padded(): after = lax.ppermute(initial, axis, down)  13 us
    gather x9, local copies, waits for them, and re-layouts  9.57 us
    psum x1, blocking collectives, on_device(): share = lax.psum(share, 'grp')  8.96 us
  transfers between devices with their start and end apart: 9, of which 5 were waited for; matrix products, arithmetic and copies ran while one was open for 1% of the time, Pallas kernels for 0%

profile of v1, /device:TPU:0, one launch (start us, length us, event | category | flops | bytes accessed | tf_op | source)
XLA Modules:
  0.0 321.5 jit_solution(2601166564011665974)
XLA Ops:
  8.3 4.9 %collective-permute-start = (f32[2,128,128]{2,1,0:T(8,128)S(1)}, f32[2,128,128]{2,1,0:T(8,128)S(1)}, u32[]{:S(2)}, u32[]{:S(2)}) collective-permute-start(f32[2,128,128]{2,1,0:T(8,128)S(1)} %get-tuple-element.352), channel_id=1, source_target_pairs={{0,16},{1,17},{2,18},{3,19},{4,20},{5,21},{6,22},{7,23},{8,24},{9,... | collective-permute-start | bytes 393224 | tf_op jit(solution)/shard_map/ppermute | solution.py:30
  13.2 1.3 collective-permute-start.1
  14.5 1.4 collective-permute-done
  15.9 1.3 constant_dynamic-update-slice_fusion.1
  17.2 2.8 collective-permute-done.1
  20.1 1.4 collective-permute-start.2
  21.5 1.3 collective-permute-start.3
  24.2 3.9 %collective-permute-done.3 = f32[2,1280,128]{2,1,0:T(8,128)} collective-permute-done((f32[2,1280,128]{2,1,0:T(8,128)S(1)}, f32[2,1280,128]{2,1,0:T(8,128)}, u32[]{:S(2)}, u32[]{:S(2)}) %collective-permute-start.3) | collective-permute-done | bytes 1310752 | tf_op jit(solution)/shard_map/ppermute | solution.py:31
  28.2 3.4 %pad_maximum_fusion = f32[2,1280,384]{2,1,0:T(8,128)} fusion(f32[2,1280,128]{2,1,0:T(8,128)} %collective-permute-done.3, f32[2,1280,128]{2,1,0:T(8,128)S(1)} %constant_dynamic-update-slice_fusion, f32[2,1280,128]{2,1,0:T(8,128)S(1)} %collective-permute-done.2), kind=kLoop, calls=%fused_computation.139 | loop fusion | flops 1966080 | bytes 7864320 | tf_op jit(solution)/shard_map/concatenate | solution.py:32
  31.7 9.6 %while.33 = (s32[]{:T(128)}, f32[2,1280,384]{2,1,0:T(8,128)}, s32[3,3]{1,0:T(4,128)S(1)}, f32[3,2,256,256]{3,2,1,0:T(8,128)S(1)}, s32[]{:T(128)}) while((s32[]{:T(128)}, f32[2,1280,384]{2,1,0:T(8,128)}, s32[3,3]{1,0:T(4,128)S(1)}, f32[3,2,256,256]{3,2,1,0:T(8,128)S(1)}, s32[]{:T(128)}) %tuple.102), condition=%wide.while_cond.4, body=%wide.while_body.4.sunk | while | flops 2 | bytes 1048693 | solution.py:86
  32.4 2.5 bitcast_dynamic-update-slice_fusion.2
  35.6 2.5 bitcast_dynamic-update-slice_fusion.2
  38.9 2.5 bitcast_dynamic-update-slice_fusion.2
  41.6 1.3 pad_maximum_fusion.1
  42.8 1.3 broadcast_in_dim.20
  44.2 30.6 %while.34 = (s32[]{:T(128)}, f32[3,2,256,256]{3,2,1,0:T(8,128)}, s32[]{:T(128)}, f32[3,2,256,256]{3,2,1,0:T(8,128)}, f32[3,256,256]{2,1,0:T(8,128)}, /*index=5*/s32[]{:T(128)}, s32[]{:T(128)}, s32[]{:T(128)}, s32[]{}) while((s32[]{:T(128)}, f32[3,2,256,256]{3,2,1,0:T(8,128)}, s32[]{:T(128)}, ...), condition=%wide.region_1.2_spmd.clone.clone, body=%wide.region_0.1_spmd.clone.clone.sunk | while | flops 3238789120 | bytes 12320939 | solution.py:102
  44.7 2.4 fusion.179
  47.2 2.4 convolution_subtract_fusion.7
  49.6 1.5 fusion.180
  51.1 2.4 fusion.181
  53.5 2.4 convolution_add_fusion.6
  56.0 1.5 convolution_subtract_fusion.8
  57.4 1.5 fusion.182
  58.9 2.4 fusion.183
  61.3 1.5 fusion.186
  62.8 1.5 convolution_add_fusion.7
  64.3 1.5 fusion.184
  65.8 1.5 convolution_subtract_fusion.9
  67.3 1.5 fusion.188
  68.7 1.5 fusion.189
  70.2 1.5 fusion.185
  71.7 1.5 fusion.187
  74.8 2.1 broadcast_in_dim.18
  76.9 14.0 %while.32 = (s32[]{:T(128)}, f32[2,1280,384]{2,1,0:T(8,128)}, f32[2,256,256]{2,1,0:T(8,128)S(1)}, s32[]{:T(128)}, s32[3]{0:T(128)S(1)}, /*index=5*/s32[3]{0:T(12...) while((s32[]{:T(128)}, f32[2,1280,384]{2,1,0:T(8,128)}, ...), condition=%wide.region_3.4_spmd, body=%wide.region_2.3_spmd.sunk | while | flops 1310731 | bytes 6816019 | solution.py:128
  82.6 1.1 fusion.161
  83.7 1.4 maximum_add_fusion.3
  85.1 5.2 %dynamic_update_slice.13 = f32[2,1280,384]{2,1,0:T(8,128)} dynamic-update-slice(f32[2,1280,384]{2,1,0:T(8,128)} %get-tuple-element.549, f32[2,256,256]{2,1,0:T(8,128)S(1)} %get-tuple-element.477, s32[]{:T(128)} %constant.180.clone.1..sunk, s32[]{:T(128)S(6)} %select_n.163, s32[]{:T(128)S(6)} %select_n.164) | dynamic-update-slice | bytes 1048580 | tf_op jit(solution)/shard_map/while/body/dynamic_update_slice | solution.py:121
  90.9 3.6 %fusion.116 = (f32[2,1280,128]{2,1,0:T(8,128)}, f32[2,1280,128]{2,1,0:T(8,128)}) fusion(f32[2,1280,384]{2,1,0:T(8,128)} %get-tuple-element.227), kind=kLoop, calls=%fused_computation.163 | loop fusion | bytes 5242880 | tf_op jit(solution)/shard_map/slice | solution.py:129
  94.5 27.6 %collective-permute-start.4 = (f32[2,1280,128]{2,1,0:T(8,128)}, f32[2,1280,128]{2,1,0:T(8,128)S(1)}, u32[]{:S(2)}, u32[]{:S(2)}) collective-permute-start(f32[2,1280,128]{2,1,0:T(8,128)} %get-tuple-element.345), channel_id=1, source_target_pairs={{0,1},{1,2},{2,3},{3,4},{4,5},{5,6},{6,7},{7,8},{8,9},{9,10},{10,1... | collective-permute-start | bytes 3932168 | tf_op jit(solution)/shard_map/ppermute | solution.py:30
  122.1 1.3 collective-permute-start.5
  124.8 146.3 %reduce-scatter.2.cloned.1.call-done = f32[2,16,256]{2,1,0:T(8,128)} async-done(((f32[2,256,256]{2,1,0:T(8,128)}), f32[2,16,256]{2,1,0:T(8,128)}) %reduce-scatter.2.cloned.1.call-update) | async-done | bytes 32784 | tf_op jit(solution)/shard_map/reduce_scatter | solution.py:141
  271.0 9.0 %psum.7 = f32[2,16,256]{2,1,0:T(8,128)S(1)} all-reduce(f32[2,16,256]{2,1,0:T(8,128)} %reduce-scatter.2.cloned.1.call-done), channel_id=1, replica_groups=mesh['grp'=2,'pos'=16] {'grp'}, use_global_device_ids=true, to_apply=%region_5.6 | all-reduce | flops 8192 | bytes 65536 | tf_op jit(solution)/shard_map/psum | solution.py:142
  280.0 1.5 add_add_fusion
  281.6 2.5 collective-permute-start.6
  284.0 20.9 %all-gather = f32[32,16,256]{2,1,0:T(8,128)S(1)} all-gather(f32[2,16,256]{2,1,0:T(8,128)S(1)} %divide_subtract_fusion), channel_id=2, replica_groups=mesh['grp'=2,'pos'=16] {'pos'}, dimensions={0}, use_global_device_ids=true | all-gather | bytes 557056 | tf_op jit(solution)/shard_map/all_gather | solution.py:15
  305.8 1.4 collective-permute-start.7
  307.3 6.3 %collective-permute-done.7 = f32[2,128,128]{2,1,0:T(8,128)S(1)} collective-permute-done((f32[2,128,128]{2,1,0:T(8,128)S(1)}, f32[2,128,128]{2,1,0:T(8,128)S(1)}, u32[]{:S(2)}, u32[]{:S(2)}) %collective-permute-start.7) | collective-permute-done | bytes 131104 | tf_op jit(solution)/shard_map/ppermute | solution.py:31
  313.6 1.1 multiply_subtract_fusion
  (47 shorter events, 8.6 us)
Async XLA Ops:
  7.2 15.6 %copy-start.4 = (s32[2,3]{1,0:T(2,128)S(1)}, s32[2,3]{1,0:T(2,128)}, u32[]{:S(2)}) copy-start(s32[2,3]{1,0:T(2,128)} %param.24) | copy-start | bytes 76
  7.2 15.7 %copy-start.5 = (s32[32]{0:T(128)S(1)}, s32[32]{0:T(128)}, u32[]{:S(2)}) copy-start(s32[32]{0:T(128)} %param.25) | copy-start | bytes 388
  7.2 16.3 %copy-start.1 = (f32[2,256,256]{2,1,0:T(8,128)S(1)}, f32[2,256,256]{2,1,0:T(8,128)}, u32[]{:S(2)}) copy-start(f32[2,256,256]{2,1,0:T(8,128)} %param.22) | copy-start | bytes 1572868
  7.2 263.8 %reduce-scatter.2.cloned.1.call-start = ((), (), s32[]{:S(2)}) async-start(), calls=%async_computation.1 | async-start | bytes 557056 | tf_op jit(solution)/shard_map/reduce_scatter | solution.py:141
  8.3 7.6 %collective-permute-start = (f32[2,128,128]{2,1,0:T(8,128)S(1)}, f32[2,128,128]{2,1,0:T(8,128)S(1)}, u32[]{:S(2)}, u32[]{:S(2)}) collective-permute-start(f32[2,128,128]{2,1,0:T(8,128)S(1)} %get-tuple-element.352), channel_id=1, source_target_pairs={{0,16},{1,17},{2,18},{3,19},{4,20},{5,21},{6,22},{7,23},{8,24},{9,... | collective-permute-start | bytes 393224 | tf_op jit(solution)/shard_map/ppermute | solution.py:30
  13.2 6.9 %collective-permute-start.1 = (f32[2,128,128]{2,1,0:T(8,128)S(1)}, f32[2,128,128]{2,1,0:T(8,128)S(1)}, u32[]{:S(2)}, u32[]{:S(2)}) collective-permute-start(f32[2,128,128]{2,1,0:T(8,128)S(1)} %get-tuple-element.351), channel_id=1, source_target_pairs={{16,0},{17,1},{18,2},{19,3},{20,4},{21,5},{22,6},{23,7},{24,8},{25... | collective-permute-start | bytes 393224 | tf_op jit(solution)/shard_map/ppermute | solution.py:31
  20.1 4.2 %collective-permute-start.2 = (f32[2,1280,128]{2,1,0:T(8,128)S(1)}, f32[2,1280,128]{2,1,0:T(8,128)S(1)}, u32[]{:S(2)}, u32[]{:S(2)}) collective-permute-start(f32[2,1280,128]{2,1,0:T(8,128)S(1)} %constant_dynamic-update-slice_fusion), channel_id=1, source_target_pairs={{0,1},{1,2},{2,3},{3,4},{4,5},{5,6},{6,7},{7,8},{8,9},{9,10},{10,1... | collective-permute-start | bytes 3932168 | tf_op jit(solution)/shard_map/ppermute | solution.py:30
  21.5 6.7 %collective-permute-start.3 = (f32[2,1280,128]{2,1,0:T(8,128)S(1)}, f32[2,1280,128]{2,1,0:T(8,128)}, u32[]{:S(2)}, u32[]{:S(2)}) collective-permute-start(f32[2,1280,128]{2,1,0:T(8,128)S(1)} %constant_dynamic-update-slice_fusion), channel_id=1, source_target_pairs={{1,0},{2,1},{3,2},{4,3},{5,4},{6,5},{7,6},{8,7},{9,8},{10,9},{11,1... | collective-permute-start | bytes 3932168 | tf_op jit(solution)/shard_map/ppermute | solution.py:31
  31.7 9.7 %copy-start.3 = (f32[256,256]{1,0:T(8,128)S(1)}, f32[256,256]{1,0:T(8,128)}, u32[]{:S(2)}) copy-start(f32[256,256]{1,0:T(8,128)} %get-tuple-element.354) | copy-start | bytes 786436
  90.9 3.6 %copy-start = (f32[2,256,256]{2,1,0:T(8,128)}, f32[2,256,256]{2,1,0:T(8,128)S(1)}, u32[]{:S(2)}) copy-start(f32[2,256,256]{2,1,0:T(8,128)S(1)} %get-tuple-element.228) | copy-start | bytes 1572868
  94.5 185.5 %collective-permute-start.4 = (f32[2,1280,128]{2,1,0:T(8,128)}, f32[2,1280,128]{2,1,0:T(8,128)S(1)}, u32[]{:S(2)}, u32[]{:S(2)}) collective-permute-start(f32[2,1280,128]{2,1,0:T(8,128)} %get-tuple-element.345), channel_id=1, source_target_pairs={{0,1},{1,2},{2,3},{3,4},{4,5},{5,6},{6,7},{7,8},{8,9},{9,10},{10,1... | collective-permute-start | bytes 3932168 | tf_op jit(solution)/shard_map/ppermute | solution.py:30
  122.1 157.9 %collective-permute-start.5 = (f32[2,1280,128]{2,1,0:T(8,128)}, f32[2,1280,128]{2,1,0:T(8,128)S(1)}, u32[]{:S(2)}, u32[]{:S(2)}) collective-permute-start(f32[2,1280,128]{2,1,0:T(8,128)} %get-tuple-element.346), channel_id=1, source_target_pairs={{1,0},{2,1},{3,2},{4,3},{5,4},{6,5},{7,6},{8,7},{9,8},{10,9},{11,1... | collective-permute-start | bytes 3932168 | tf_op jit(solution)/shard_map/ppermute | solution.py:31
  281.6 25.7 %collective-permute-start.6 = (f32[2,128,128]{2,1,0:T(8,128)S(1)}, f32[2,128,128]{2,1,0:T(8,128)S(1)}, u32[]{:S(2)}, u32[]{:S(2)}) collective-permute-start(f32[2,128,128]{2,1,0:T(8,128)S(1)} %get-tuple-element.350), channel_id=1, source_target_pairs={{0,16},{1,17},{2,18},{3,19},{4,20},{5,21},{6,22},{7,23},{8,24},{9,... | collective-permute-start | bytes 393224 | tf_op jit(solution)/shard_map/ppermute | solution.py:30
  305.7 7.9 %copy-start.2 = (f32[2,1024,128]{2,1,0:T(8,128)S(1)}, f32[2,1024,128]{2,1,0:T(8,128)}, u32[]{:S(2)}) copy-start(f32[2,1024,128]{2,1,0:T(8,128)} %param.21) | copy-start | bytes 3145732
  305.8 7.8 %collective-permute-start.7 = (f32[2,128,128]{2,1,0:T(8,128)S(1)}, f32[2,128,128]{2,1,0:T(8,128)S(1)}, u32[]{:S(2)}, u32[]{:S(2)}) collective-permute-start(f32[2,128,128]{2,1,0:T(8,128)S(1)} %get-tuple-element.349), channel_id=1, source_target_pairs={{16,0},{17,1},{18,2},{19,3},{20,4},{21,5},{22,6},{23,7},{24,8},{25... | collective-permute-start | bytes 393224 | tf_op jit(solution)/shard_map/ppermute | solution.py:31
Sparse Core Ops, SparseCore 0:
  123.6 147.3 reduce-scatter.1
